TPU v7x, 512 devices: a whole 4x4x16 slice. The times are simulated.
512 devices in a mesh: grp: 64 (over x, z), box: 8 (over y, core).
Axes of the slice: x: 4, y: 4, z: 16, core: 2. Of those that a mesh axis runs over, the one named last changes fastest.
Arguments:
- fine_state: float32 [64, 5, 32, 16, 256], P('grp', None, 'box'), may hold values from -1 to 6, as said below
- patch_ghosts: float32 [64, 2, 2, 5, 16, 256], P('grp'), may hold values from -1 to 6, as said below
- coarse_state: float32 [64, 8, 24, 5, 128], P('grp', 'box'), may hold values from -1 to 6, as said below
- coarse_face_term: float32 [64, 8, 24, 5, 128], P('grp', 'box'), may hold values from -1 to 1
- dest_grp: int32 [64, 8, 24], P('grp', 'box'), may hold values from 0 to 63, as said below
- dest_column: int32 [64, 8, 24], P('grp', 'box'), may hold values from 0 to 23, as said below
Outputs:
- fine_new: float32 [64, 5, 32, 16, 256], P('grp', None, 'box')
- coarse_new: float32 [64, 8, 24, 5, 128], P('grp', 'box')
Inputs may be any that keep to these rules, and one draw needn't show every extreme that they name: `fine_state`: every cell has density in 1 to 2, velocity components in -0.5 to 0.5 and pressure in 1 to 2. `patch_ghosts`: every cell has density in 1 to 2, velocity components in -0.5 to 0.5 and pressure in 1 to 2. `coarse_state`: every cell has density in 1 to 2, velocity components in -0.5 to 0.5 and pressure in 1 to 2. `dest_grp`: for each box index, each owner's columns receive exactly one record each; one box sends at most 1 and at least 0 records to each owner. `dest_column`: see dest_grp.
All inputs are finite; a program needn't handle non-finite values.
Results may differ from a plain program's by a relative error of at most 0.0001.
Values sent between devices are 32-bit elements; how exact they have to be, the bound alone decides.
A program may use at most 64 MiB of HBM per device.

v0:
```python
import jax
import jax.numpy as jnp
from jax import lax
from jax.sharding import PartitionSpec as P

gamma_ratio = 1.4
time_step = 0.06


def extended_2(cells, sides, width):
    for axis, dim in sides:
        count = lax.axis_size(axis)
        ends = count - 1
        head = lax.slice_in_dim(cells, 0, width, axis=dim)
        tail = lax.slice_in_dim(cells, cells.shape[dim] - width, cells.shape[dim], axis=dim)
        cells = jnp.concatenate(
            [
                lax.ppermute(tail, axis, [(i, (i + 1) % count) for i in range(ends)]),
                cells,
                lax.ppermute(head, axis, [((i + 1) % count, i) for i in range(ends)]),
            ],
            axis=dim,
        )
    return cells


def side_by_side(arrays, axis, split_dim, concat_dim, along):
    columns = [a.reshape(*a.shape[:along], -1) for a in arrays]
    both = jnp.concatenate(columns, axis=along)
    out, at, done = (
        lax.all_to_all(both, axis, split_axis=split_dim, concat_axis=concat_dim, tiled=True),
        0,
        [],
    )
    for a, column in zip(arrays, columns):
        section = out[..., at : at + column.shape[along]]
        done.append(section.reshape(*section.shape[:along], *a.shape[along:]))
        at += column.shape[along]
    return tuple(done)


def cell_values(conserved):
    density = conserved[0]
    velocity = conserved[1:4] / density
    kinetic = 0.5 * jnp.sum(conserved[1:4] * velocity, axis=0)
    pressure = (gamma_ratio - 1.0) * (conserved[4] - kinetic)
    sound_speed = jnp.sqrt(gamma_ratio * pressure / density)
    return (velocity, pressure, sound_speed)


def physical_flux(conserved, velocity, pressure, normal):
    moving = velocity[normal]
    pieces = [conserved[1 + normal]]
    for member in range(3):
        if member == normal:
            pieces.append(conserved[1 + member] * moving + pressure)
        else:
            pieces.append(conserved[1 + member] * moving)
    pieces.append((conserved[4] + pressure) * moving)
    return jnp.stack(pieces)


def rusanov(left_state, right_state, left_flux, right_flux, left_speed, right_speed):
    biggest = jnp.maximum(left_speed, right_speed)
    return 0.5 * (left_flux + right_flux) - 0.5 * biggest * (right_state - left_state)


def advance(extended):
    velocity, pressure, sound_speed = cell_values(extended)
    cell_flux = physical_flux(extended, velocity, pressure, 0)
    cell_speed = jnp.abs(velocity[0]) + sound_speed
    face_flux = rusanov(
        extended[:, :-1],
        extended[:, 1:],
        cell_flux[:, :-1],
        cell_flux[:, 1:],
        cell_speed[:-1],
        cell_speed[1:],
    )
    interior = extended[:, 1:-1]
    change = face_flux[:, 1:] - face_flux[:, :-1]
    inner_velocity = velocity[:, 1:-1]
    inner_pressure = pressure[1:-1]
    inner_sound = sound_speed[1:-1]
    for normal in (1, 2):
        side_flux = physical_flux(interior, inner_velocity, inner_pressure, normal)
        side_speed = jnp.abs(inner_velocity[normal]) + inner_sound
        grid_axis = normal + 1
        face_values = rusanov(
            interior,
            jnp.roll(interior, -1, grid_axis),
            side_flux,
            jnp.roll(side_flux, -1, grid_axis),
            side_speed,
            jnp.roll(side_speed, -1, normal),
        )
        change = change + (face_values - jnp.roll(face_values, 1, grid_axis))
    return (interior - time_step * change, face_flux)


def on_device(fine_state, patch_ghosts, coarse_state, coarse_face_term, dest_grp, dest_column):
    box_count = lax.axis_size("box")
    box_place = lax.axis_index("box")
    at_low = box_place == 0
    at_high = box_place == box_count - 1
    current = fine_state[0]
    ghosts = patch_ghosts[0]
    fields, cells_along, cells_across, cells_depth = current.shape

    def with_ghosts(extended, width, time_frac):
        ghost_low = (1.0 - time_frac) * ghosts[0, 0] + time_frac * ghosts[1, 0]
        ghost_high = (1.0 - time_frac) * ghosts[0, 1] + time_frac * ghosts[1, 1]
        edge_shape = (fields, width, cells_across, cells_depth)
        lower = jnp.where(
            at_low, jnp.broadcast_to(ghost_low[:, None], edge_shape), extended[:, :width]
        )
        upper = jnp.where(
            at_high, jnp.broadcast_to(ghost_high[:, None], edge_shape), extended[:, -width:]
        )
        return jnp.concatenate([lower, extended[:, width:-width], upper], axis=1)

    extended = extended_2(current, (("box", 1),), 2)
    halfway, first_flux = advance(with_ghosts(extended, 2, 0.0))
    updated, second_flux = advance(with_ghosts(halfway, 1, 0.5))
    low_sum = first_flux[:, 1] + second_flux[:, 0]
    high_sum = first_flux[:, -2] + second_flux[:, -1]
    coarse_rows = cells_along // 2
    coarse_cols = cells_across // 2
    coarse_depth = cells_depth // 2
    averaged = updated.reshape(fields, coarse_rows, 2, coarse_cols, 2, coarse_depth, 2).mean(
        axis=(2, 4, 6)
    )
    avg_records = averaged.transpose(1, 2, 0, 3).reshape(
        coarse_rows * coarse_cols, fields, coarse_depth
    )
    face_sum = jnp.where(at_low, low_sum, high_sum)
    face_coarse = (
        face_sum.reshape(fields, coarse_cols, 2, coarse_depth, 2)
        .sum(axis=(2, 4))
        .transpose(1, 0, 2)
    )
    flux_records = jnp.where(at_low, -time_step / 8, time_step / 8) * face_coarse
    records = jnp.concatenate([avg_records, flux_records], axis=0)
    count_average = coarse_rows * coarse_cols
    total = count_average + coarse_cols
    is_live = jnp.concatenate(
        [jnp.ones((count_average,), bool), jnp.broadcast_to(at_low | at_high, (coarse_cols,))]
    )
    kind_sign = jnp.concatenate(
        [jnp.ones((count_average,), jnp.float32), -jnp.ones((coarse_cols,), jnp.float32)]
    )
    owners = dest_grp[0, 0]
    columns = dest_column[0, 0]
    group_count = lax.axis_size("grp")
    capacity = (total + group_count - 1) // group_count
    record_ids = jnp.arange(total, dtype=jnp.int32)
    same_owner = owners[:, None] == owners[None, :]
    earlier = record_ids[None, :] < record_ids[:, None]
    position = jnp.sum((same_owner & earlier).astype(jnp.int32), axis=1)
    slot_code = jnp.where(is_live, (columns + 1).astype(jnp.float32) * kind_sign, 0.0)
    outgoing = (
        jnp.zeros((group_count, capacity, fields, coarse_depth), jnp.float32)
        .at[owners, position]
        .set(records)
    )
    out_codes = jnp.zeros((group_count, capacity), jnp.float32).at[owners, position].set(slot_code)
    incoming, in_codes = side_by_side((outgoing, out_codes), "grp", 0, 0, 2)
    flat = incoming.reshape(group_count * capacity, fields * coarse_depth)
    codes = in_codes.reshape(group_count * capacity)
    targets = (record_ids + 1).astype(jnp.float32)
    avg_hot = (codes[None, :] == targets[:, None]).astype(jnp.float32)
    face_hot = (codes[None, :] == -targets[:, None]).astype(jnp.float32)
    values = jnp.dot(
        avg_hot + face_hot,
        flat,
        precision=lax.Precision.HIGHEST,
        preferred_element_type=jnp.float32,
    ).reshape(total, fields, coarse_depth)
    avg_flag = jnp.sum(avg_hot, axis=1)
    face_flag = jnp.sum(face_hot, axis=1)
    coarse_new = jnp.where(
        avg_flag[:, None, None] > 0,
        values,
        coarse_state[0, 0] + face_flag[:, None, None] * (values - coarse_face_term[0, 0]),
    )
    return (updated[None], coarse_new[None, None])


def solution(mesh):
    in_specs = (
        P("grp", None, "box", None, None),
        P("grp", None, None, None, None, None),
        P("grp", "box", None, None, None),
        P("grp", "box", None, None, None),
        P("grp", "box", None),
        P("grp", "box", None),
    )
    out_specs = (P("grp", None, "box", None, None), P("grp", "box", None, None, None))
    return jax.shard_map(
        on_device, mesh=mesh, in_specs=in_specs, out_specs=out_specs, check_vma=False
    )
```

profile of v0, /device:TPU:1, one launch (start us, length us, event | category | flops | bytes accessed | tf_op | source)
XLA Modules:
  0.0 80.6 jit_solution(2298929209755965016)
XLA Ops:
  0.6 1.0 %fusion.74 = (f32[5,2,16,256]{3,2,1,0:T(8,128)S(1)}, f32[5,2,16,256]{3,2,1,0:T(8,128)S(1)}) fusion(f32[5,4,16,256]{3,2,1,0:T(8,128)} %bitcast.208), kind=kLoop, calls=%fused_computation.184 | loop fusion | bytes 655360 | tf_op jit(solution)/shard_map/slice | solution.py:15
  1.7 8.7 %collective-permute-start.1 = (f32[5,2,16,256]{3,2,1,0:T(8,128)S(1)}, f32[5,2,16,256]{3,2,1,0:T(8,128)S(1)}, u32[]{:S(2)}, u32[]{:S(2)}) collective-permute-start(f32[5,2,16,256]{3,2,1,0:T(8,128)S(1)} %get-tuple-element.45), channel_id=1, source_target_pairs={{1,0},{2,1},{3,2},{4,3},{5,4},{6,5},{7,6},{9,8},{10,9},{11,10},{12... | collective-permute-start | bytes 491528 | tf_op jit(solution)/shard_map/ppermute | solution.py:20
  10.4 1.9 %collective-permute-start = (f32[5,2,16,256]{3,2,1,0:T(8,128)S(1)}, f32[5,2,16,256]{3,2,1,0:T(8,128)S(1)}, u32[]{:S(2)}, u32[]{:S(2)}) collective-permute-start(f32[5,2,16,256]{3,2,1,0:T(8,128)S(1)} %get-tuple-element.44), channel_id=1, source_target_pairs={{0,1},{1,2},{2,3},{3,4},{4,5},{5,6},{6,7},{8,9},{9,10},{10,11},{11... | collective-permute-start | bytes 491528 | tf_op jit(solution)/shard_map/ppermute | solution.py:18
  12.3 0.9 %convert_reduce_fusion.2 = s32[24]{0:T(128)S(1)} fusion(s32[24]{0:T(128)} %bitcast.217), kind=kLoop, calls=%fused_computation.168 | loop fusion | flops 2856 | bytes 192 | tf_op jit(solution)/shard_map/reduce_sum | solution.py:159
  13.3 0.7 fusion.70
  13.9 0.7 pad_select_fusion
  14.6 0.6 scatter_custom_fusion.1
  15.3 0.1 copy.51
  15.4 0.0 copy-start
  15.4 1.1 %add_bitcast_fusion.1 = (f32[5,16,256]{2,1,0:T(8,128)S(1)}, f32[5,16,256]{2,1,0:T(8,128)S(1)}) fusion(f32[2,2,5,16,256]{4,3,2,1,0:T(8,128)} %bitcast.212), kind=kLoop, calls=%fused_computation.129 | loop fusion | flops 81920 | bytes 491520 | tf_op jit(solution)/shard_map/add | solution.py:111
  16.4 0.0 collective-permute-done.1
  16.5 0.0 collective-permute-done
  16.5 1.0 %pad_maximum_fusion = f32[5,8,16,256]{3,2,1,0:T(8,128)S(1)} fusion(f32[5,2,16,256]{3,2,1,0:T(8,128)S(1)} %broadcast_select_fusion, f32[5,4,16,256]{3,2,1,0:T(8,128)} %bitcast.209, f32[5,2,16,256]{3,2,1,0:T(8,128)S(1)} %broadcast_select_fusion.1), kind=kLoop, calls=%fused_computation.3 | loop fusion | flops 327680 | bytes 1310720 | tf_op jit(solution)/shard_map/concatenate | solution.py:120
  17.6 0.1 multiply_reduce_fusion
  17.7 0.1 bitcast_add_fusion
  18.0 0.2 slice.487
  18.2 0.2 slice.491
  18.4 0.1 slice.489
  18.7 0.0 copy-start.2
  18.8 0.1 fusion.38
  18.9 0.0 copy-done
  18.9 0.5 fusion.13
  19.5 0.1 slice.493
  19.6 0.2 fusion.1
  19.8 0.4 fusion.10
  20.2 0.0 copy-done.2
  20.4 0.1 bitcast_add_fusion.1
  20.6 0.1 slice.527
  20.8 0.1 slice.531
  21.0 0.1 slice.529
  21.3 0.1 fusion.51
  21.4 0.3 fusion.26
  21.8 0.1 slice.533
  21.9 0.9 %fusion.16 = f32[5,5,16,256]{3,2,1,0:T(8,128)} fusion(f32[5,6,16,256]{3,2,1,0:T(8,128)S(1)} %multiply_dynamic-update-slice_fusion.1, f32[5,1,16,256]{3,2,1,0:T(8,128)S(1)} %slice_select_fusion, f32[5,4,16,256]{3,2,1,0:T(8,128)S(1)} %slice.495, f32[5,1,16,256]{3,2,1,0:T(8,128)S(1)} %fusion.48, f32[5,16,256]{2,1,0:T(8,128)S(1)} %fusion.46), kind=kLoop, calls=%fused_computation.33 | loop fusion | flops 716800 | bytes 1802240 | tf_op jit(solution)/shard_map/sub | solution.py:65
  22.8 1.0 %fusion.45 = f32[5,1,16,256]{3,2,1,0:T(8,128)S(1)} fusion(f32[5,5,16,256]{3,2,1,0:T(8,128)} %fusion.16, f32[5,7,16,256]{3,2,1,0:T(8,128)S(1)} %fusion.1, pred[]{:T(512)S(6)} %eq.47), kind=kLoop, calls=%fused_computation.118 | loop fusion | flops 61440 | bytes 409601 | tf_op jit(solution)/shard_map/jit(_where)/select_n | solution.py:136
  23.7 0.7 copy.48
  24.4 2.8 %reduce_sum.70 = f32[5,8,128]{0,2,1:T(8,128)} reduce(f32[5,8,2,128,2]{0,4,3,2,1:T(2,128)S(1)} %bitcast.203, f32[]{:T(128)} %constant.17.clone.1), dimensions={2,4}, to_apply=%region_4.5 | reduce | flops 15360 | bytes 102404 | tf_op jit(solution)/shard_map/reduce_sum | solution.py:139
  27.2 1.1 %multiply_bitcast_fusion.1 = f32[8,5,128]{1,2,0:T(8,128)S(1)} fusion(f32[5,8,128]{0,2,1:T(8,128)} %reduce_sum.70, f32[]{:T(128)S(6)} %select_n.86), kind=kLoop, calls=%fused_computation.9 | loop fusion | flops 5120 | bytes 40964 | tf_op jit(solution)/shard_map/mul | solution.py:142
  28.3 0.2 copy.49
  28.5 1.3 %fusion.21 = f32[5,4,16,256]{3,2,1,0:T(8,128)S(1)} fusion(f32[5,5,16,256]{3,2,1,0:T(8,128)} %fusion.16, f32[5,4,16,256]{3,2,1,0:T(8,128)S(1)} %get-tuple-element.35, f32[5,4,15,256]{3,2,1,0:T(8,128)S(1)} %bitcast.207, f32[5,4,1,256]{3,2,1,0:T(1,128)S(1)} %slice.524, f32[5,4,16,256]{3,2,1,0:T(8,128)S(1)} %get-tuple-element.34, ...), kind=kLoop, calls=%fused_computation.42 | loop fusion | flops 737280 | bytes 2621440 | tf_op jit(solution)/shard_map/sub | solution.py:98
  29.8 0.0 copy-start.1
  29.8 4.9 %copy.45 = f32[5,4,16,256]{0,3,2,1:T(8,128)} copy(f32[5,4,16,256]{3,2,1,0:T(8,128)S(1)} %fusion.21) | data formatting | bytes 655360 | tf_op jit(solution)/shard_map/sub | solution.py:98
  34.7 0.0 copy-start.3
  34.7 0.0 copy-start.4
  34.7 8.7 %reduce_sum.69 = f32[5,2,8,128]{0,3,2,1:T(8,128)S(1)} reduce(f32[5,2,2,8,2,128,2]{0,6,5,4,3,2,1:T(2,128)} %bitcast.202, f32[]{:T(128)} %constant.17.clone.1), dimensions={2,4,6}, to_apply=%region_3.4 | reduce | flops 71680 | bytes 368644 | tf_op jit(solution)/shard_map/reduce_sum | solution.py:130
  43.4 0.0 copy-done.1
  43.4 0.1 multiply_bitcast_fusion
  43.5 0.3 copy.46
  43.9 1.5 %scatter_fusion = f32[64,5,128]{2,1,0:T(8,128)S(1)} fusion(f32[64,5,128]{2,1,0:T(8,128)S(1)} %broadcast.172, s32[24]{0:T(128)S(1)} %fusion.70, f32[24,5,128]{2,1,0:T(8,128)S(1)} %copy.50), kind=kCustom, calls=%fused_computation | custom fusion | bytes 184416 | tf_op jit(solution)/shard_map/scatter | solution.py:164
  45.5 0.9 %copy.52 = f32[64,1,641]{2,1,0:T(1,128)} copy(f32[64,1,641]{2,0,1:T(8,128)S(1)} %pad_maximum_fusion.4) | data formatting | bytes 328192 | tf_op jit(solution)/shard_map/concatenate | solution.py:29
  46.4 14.1 %all-to-all-start = ((f32[64,1,641]{2,1,0:T(1,128)}), f32[64,1,641]{2,1,0:T(1,128)S(1)}, u32[]{:S(2)}, u32[]{:S(2)}) async-start(f32[64,1,641]{2,1,0:T(1,128)} %copy.52), calls=%async_computation | async-start | bytes 393216 | tf_op jit(solution)/shard_map/all_to_all | solution.py:31
  60.5 18.4 %all-to-all-done = f32[64,1,641]{2,1,0:T(1,128)S(1)} async-done(((f32[64,1,641]{2,1,0:T(1,128)}), f32[64,1,641]{2,1,0:T(1,128)S(1)}, u32[]{:S(2)}, u32[]{:S(2)}) %all-to-all-start) | async-done | bytes 164128 | tf_op jit(solution)/shard_map/all_to_all | solution.py:31
  78.9 0.6 slice_reduce_fusion
  79.4 0.2 convert_reduce_fusion.1
  79.7 0.0 copy-done.3
  79.7 0.0 copy-done.4
  79.7 0.9 %fusion.61 = f32[1,1,24,5,128]{4,2,3,1,0:T(8,128)} fusion(f32[1,1,24,5,128]{4,2,3,1,0:T(8,128)S(1)} %copy-done.3, f32[1,1,24,5,128]{4,2,3,1,0:T(8,128)S(1)} %copy-done.4, f32[24]{0:T(128)S(1)} %get-tuple-element.3, pred[24]{0:T(512)(128)(4,1)S(1)} %broadcast_compare_fusion, f32[64]{0:T(128)S(1)} %slice_reduce_fusion, f32[24]{0:T(128)S(1)} %fusion.73, ...), kind=kOutput, calls=%fused_computation.162 | convolution fusion | flops 11865600 | bytes 348728 | tf_op jit(solution)/shard_map/dot_general | solution.py:173
  (63 shorter events, 1.3 us)
Async XLA Ops:
  1.7 14.8 %collective-permute-start.1 = (f32[5,2,16,256]{3,2,1,0:T(8,128)S(1)}, f32[5,2,16,256]{3,2,1,0:T(8,128)S(1)}, u32[]{:S(2)}, u32[]{:S(2)}) collective-permute-start(f32[5,2,16,256]{3,2,1,0:T(8,128)S(1)} %get-tuple-element.45), channel_id=1, source_target_pairs={{1,0},{2,1},{3,2},{4,3},{5,4},{6,5},{7,6},{9,8},{10,9},{11,10},{12... | collective-permute-start | bytes 491528 | tf_op jit(solution)/shard_map/ppermute | solution.py:20
  10.4 6.1 %collective-permute-start = (f32[5,2,16,256]{3,2,1,0:T(8,128)S(1)}, f32[5,2,16,256]{3,2,1,0:T(8,128)S(1)}, u32[]{:S(2)}, u32[]{:S(2)}) collective-permute-start(f32[5,2,16,256]{3,2,1,0:T(8,128)S(1)} %get-tuple-element.44), channel_id=1, source_target_pairs={{0,1},{1,2},{2,3},{3,4},{4,5},{5,6},{6,7},{8,9},{9,10},{10,11},{11... | collective-permute-start | bytes 491528 | tf_op jit(solution)/shard_map/ppermute | solution.py:18
  15.4 3.6 %copy-start = (f32[1,5,4,16,256]{4,3,2,1,0:T(8,128)S(1)}, f32[1,5,4,16,256]{4,3,2,1,0:T(8,128)}, u32[]{:S(2)}) copy-start(f32[1,5,4,16,256]{4,3,2,1,0:T(8,128)} %param.6) | copy-start | bytes 983044
  18.7 1.5 %copy-start.2 = (f32[1,2,2,5,16,256]{5,4,3,2,1,0:T(8,128)S(1)}, f32[1,2,2,5,16,256]{5,4,3,2,1,0:T(8,128)}, u32[]{:S(2)}) copy-start(f32[1,2,2,5,16,256]{5,4,3,2,1,0:T(8,128)} %param.7) | copy-start | bytes 983044
  29.8 13.6 %copy-start.1 = (f32[5,4,16,256]{3,2,1,0:T(8,128)}, f32[5,4,16,256]{3,2,1,0:T(8,128)S(1)}, u32[]{:S(2)}) copy-start(f32[5,4,16,256]{3,2,1,0:T(8,128)S(1)} %fusion.21) | copy-start | bytes 983044
  34.7 45.0 %copy-start.3 = (f32[1,1,24,5,128]{4,2,3,1,0:T(8,128)S(1)}, f32[1,1,24,5,128]{4,2,3,1,0:T(8,128)}, u32[]{:S(2)}) copy-start(f32[1,1,24,5,128]{4,2,3,1,0:T(8,128)} %param.9) | copy-start | bytes 184324
  34.7 45.0 %copy-start.4 = (f32[1,1,24,5,128]{4,2,3,1,0:T(8,128)S(1)}, f32[1,1,24,5,128]{4,2,3,1,0:T(8,128)}, u32[]{:S(2)}) copy-start(f32[1,1,24,5,128]{4,2,3,1,0:T(8,128)} %param.8) | copy-start | bytes 184324
  46.4 32.5 %all-to-all-start = ((f32[64,1,641]{2,1,0:T(1,128)}), f32[64,1,641]{2,1,0:T(1,128)S(1)}, u32[]{:S(2)}, u32[]{:S(2)}) async-start(f32[64,1,641]{2,1,0:T(1,128)} %copy.52), calls=%async_computation | async-start | bytes 393216 | tf_op jit(solution)/shard_map/all_to_all | solution.py:31
where the time goes:
time: 81 us; the launch traced here: 80.6 us
  starting transfers between devices  24.8 us (31%)
  other arithmetic  22.8 us (28%)
  waiting for transfers between devices  18.4 us (23%)
  local copies, waits for them, and re-layouts  12.4 us (15%)
  between operations  1.32 us (2%)
  matrix products  0.91 us (1%)
    all_to_all x1, waiting for transfers between devices, side_by_side(): lax.all_to_all(both, axis, split_axis=split_dim, concat_axis=concat_dim,...  18.4 us
    all_to_all x1, starting transfers between devices, side_by_side(): lax.all_to_all(both, axis, split_axis=split_dim, concat_axis=concat_dim,...  14.1 us
    ppermute x1, starting transfers between devices, extended_2(): lax.ppermute(head, axis, [((i + 1) % count, i) for i in range(ends)])  8.75 us
    reduce_sum x1, other arithmetic, on_device(): updated.reshape(fields, coarse_rows, 2, coarse_cols, 2, coarse_depth, 2)  8.66 us
    sub x1, local copies, waits for them, and re-layouts, advance(): return (interior - time_step * change, face_flux)  4.88 us
    reduce_sum x1, other arithmetic, on_device(): face_coarse = face_sum.reshape(fields, coarse_cols, 2, coarse_depth, 2).s...  2.81 us
    ppermute x1, starting transfers between devices, extended_2(): lax.ppermute(tail, axis, [(i, (i + 1) % count) for i in range(ends)])  1.92 us
    sub x4, other arithmetic, rusanov(): 0.5 * (left_flux + right_flux) - 0.5 * biggest * (right_state - left_state)  1.85 us
  transfers between devices with their start and end apart: 3, of which 1 were waited for; matrix products, arithmetic and copies ran while one was open for 5% of the time, Pallas kernels for 0%

commit v1 on v0

v1 whole, which is shorter than its diff:
```python
import functools

import jax
import jax.numpy as jnp
from jax import lax
from jax.experimental import pallas as pl
from jax.experimental.pallas import tpu as pltpu
from jax.sharding import PartitionSpec as P

MESH = pl.DeviceIdType.MESH
HALF_STEP = 0.03
NX, NZ, NB = 4, 16, 8
F = 5


def primitives(u):
    inverse = 1.0 / u[0]
    v = [u[1] * inverse, u[2] * inverse, u[3] * inverse]
    kinetic = 0.5 * (u[1] * v[0] + u[2] * v[1] + u[3] * v[2])
    pressure = 0.4 * (u[4] - kinetic)
    sound = jnp.sqrt(1.4 * pressure * inverse)
    return v + [pressure, sound]


def flux(u, q, d):
    out = [u[1 + d]]
    for m in range(3):
        f = u[1 + m] * q[d]
        out.append(f + q[3] if m == d else f)
    out.append((u[4] + q[3]) * q[d])
    return out


def kernel(
    fine, ghosts, state, term, dgrp, dcol,
    fine_out, coarse_out,
    ext, mid, q1, q2, fx, fnew, gbuf, face_sum, sums, rec, slots, recv,
    code_tx, code_rx, idx_v, state_v, term_v, coarse_v,
    dg_s, dc_s, inv_s, src_s,
    in_sem, halo_s, halo_r, code_s, code_r, rec_s, rec_r,
):
    me = lax.axis_index("grp")
    box = lax.axis_index("box")
    at_low = box == 0
    at_high = box == NB - 1
    mx, mz = lax.div(me, NZ), lax.rem(me, NZ)

    offsets = [(dx, dz) for dx in range(NX) for dz in range(NZ) if (dx, dz) != (0, 0)]
    offsets.sort(key=lambda o: -(min(o[0], NX - o[0]) + min(o[1], NZ - o[1])))

    def peer(o):
        return lax.rem(mx + o[0], NX) * NZ + lax.rem(mz + o[1], NZ)

    barrier = pltpu.get_barrier_semaphore()
    for o in offsets:
        pl.semaphore_signal(barrier, inc=1, device_id={"grp": peer(o)}, device_id_type=MESH)

    @pl.when(jnp.logical_not(at_low))
    def _():
        pl.semaphore_signal(barrier, inc=1, device_id={"box": box - 1}, device_id_type=MESH)

    @pl.when(jnp.logical_not(at_high))
    def _():
        pl.semaphore_signal(barrier, inc=1, device_id={"box": box + 1}, device_id_type=MESH)

    load_fine = pltpu.make_async_copy(fine.at[0], ext.at[:, pl.ds(2, 4)], in_sem.at[0])
    load_dg = pltpu.make_async_copy(dgrp, dg_s, in_sem.at[1])
    load_dc = pltpu.make_async_copy(dcol, dc_s, in_sem.at[2])
    load_state = pltpu.make_async_copy(state.at[0, 0], state_v, in_sem.at[3])
    load_term = pltpu.make_async_copy(term.at[0, 0], term_v, in_sem.at[4])
    load_dg.start()
    load_dc.start()
    load_fine.start()

    def ghost_loads(side):
        near, far = (1, 0) if side == 0 else (6, 7)
        return [
            pltpu.make_async_copy(ghosts.at[0, 0, side], ext.at[:, near], in_sem.at[5]),
            pltpu.make_async_copy(ghosts.at[0, 0, side], ext.at[:, far], in_sem.at[6]),
            pltpu.make_async_copy(ghosts.at[0, 1, side], gbuf, in_sem.at[7]),
        ]

    @pl.when(at_low)
    def _():
        for c in ghost_loads(0):
            c.start()

    @pl.when(at_high)
    def _():
        for c in ghost_loads(1):
            c.start()

    load_state.start()
    load_term.start()

    lane = lax.broadcasted_iota(jnp.int32, (1, 128), 1)
    load_dg.wait()
    load_dc.wait()
    live_face = jnp.where(at_low | at_high, 1, 0)
    which = jnp.full((1, 128), 24, jnp.int32)
    code = jnp.zeros((1, 128), jnp.int32)
    for r in range(24):
        hit = lane == dg_s[0, 0, r]
        which = jnp.where(hit, r, which)
        value = dc_s[0, 0, r] + 1
        if r >= 16:
            value = (value + 32) * live_face
        code = jnp.where(hit, value, code)
    code_tx[...] = code.astype(jnp.float32)
    idx_v[0] = which
    to_inv = pltpu.make_async_copy(idx_v.at[0], inv_s, in_sem.at[8])
    to_inv.start()

    load_fine.wait()
    neighbours = jnp.where(at_low | at_high, 1, 2)
    pl.semaphore_wait(barrier, 63 + neighbours)

    def halo_down():
        return pltpu.make_async_remote_copy(
            ext.at[:, pl.ds(2, 2)], ext.at[:, pl.ds(6, 2)], halo_s.at[0], halo_r.at[0],
            device_id={"box": box - 1}, device_id_type=MESH,
        )

    def halo_up():
        return pltpu.make_async_remote_copy(
            ext.at[:, pl.ds(4, 2)], ext.at[:, pl.ds(0, 2)], halo_s.at[1], halo_r.at[1],
            device_id={"box": box + 1}, device_id_type=MESH,
        )

    @pl.when(jnp.logical_not(at_low))
    def _():
        halo_down().start()

    @pl.when(jnp.logical_not(at_high))
    def _():
        halo_up().start()

    def code_copy(o):
        p = peer(o)
        return pltpu.make_async_remote_copy(
            code_tx, code_rx.at[me], code_s, code_r, device_id={"grp": p}, device_id_type=MESH
        )

    for o in offsets:
        code_copy(o).start()
    code_rx[me] = code_tx[...]

    def prim_plane(u_ref, q_ref, i):
        q = primitives([u_ref[f, i] for f in range(F)])
        for f in range(F):
            q_ref[f, i] = q[f]

    def face_plane(u_ref, q_ref, i):
        ul, ur = [u_ref[f, i] for f in range(F)], [u_ref[f, i + 1] for f in range(F)]
        ql, qr = [q_ref[f, i] for f in range(F)], [q_ref[f, i + 1] for f in range(F)]
        fl, fr = flux(ul, ql, 0), flux(ur, qr, 0)
        biggest = jnp.maximum(jnp.abs(ql[0]) + ql[4], jnp.abs(qr[0]) + qr[4])
        for f in range(F):
            fx[f, i] = (fl[f] + fr[f]) - biggest * (ur[f] - ul[f])

    def update_plane(u_ref, q_ref, i, dst, j):
        u = [u_ref[f, i] for f in range(F)]
        q = [q_ref[f, i] for f in range(F)]
        change = [fx[f, i] - fx[f, i - 1] for f in range(F)]
        for d, axis, size in ((1, 0, 16), (2, 1, 256)):
            fl = flux(u, q, d)
            s = jnp.abs(q[d]) + q[4]
            biggest = jnp.maximum(s, pltpu.roll(s, size - 1, axis))
            for f in range(F):
                up, fp = pltpu.roll(u[f], size - 1, axis), pltpu.roll(fl[f], size - 1, axis)
                face = (fl[f] + fp) - biggest * (up - u[f])
                change[f] = change[f] + (face - pltpu.roll(face, 1, axis))
        for f in range(F):
            dst[f, j] = u[f] - HALF_STEP * change[f]

    def loop(lo, hi, body):
        def step(i, carry):
            body(i)
            return carry

        lax.fori_loop(lo, hi, step, 0)

    loop(2, 6, lambda i: prim_plane(ext, q1, i))
    loop(2, 5, lambda i: face_plane(ext, q1, i))
    loop(3, 5, lambda i: update_plane(ext, q1, i, mid, i))

    @pl.when(jnp.logical_not(at_low))
    def _():
        halo_down().wait_send()
        halo_up().wait_recv()

    @pl.when(at_low)
    def _():
        for c in ghost_loads(0):
            c.wait()

    @pl.when(jnp.logical_not(at_high))
    def _():
        halo_up().wait_send()
        halo_down().wait_recv()

    @pl.when(at_high)
    def _():
        for c in ghost_loads(1):
            c.wait()

    loop(0, 2, lambda i: prim_plane(ext, q1, i))
    loop(6, 8, lambda i: prim_plane(ext, q1, i))
    loop(0, 2, lambda i: face_plane(ext, q1, i))
    loop(5, 7, lambda i: face_plane(ext, q1, i))
    loop(1, 3, lambda i: update_plane(ext, q1, i, mid, i))
    loop(5, 7, lambda i: update_plane(ext, q1, i, mid, i))

    scale = jnp.where(at_low, -0.0075 * 0.5, 0.0075 * 0.5)
    edge = jnp.where(at_low, 1, 5)
    for f in range(F):
        face_sum[f] = fx[f, edge]

    @pl.when(at_low)
    def _():
        for f in range(F):
            mid[f, 1] = 0.5 * ext[f, 1] + 0.5 * gbuf[f]

    @pl.when(at_high)
    def _():
        for f in range(F):
            mid[f, 6] = 0.5 * ext[f, 6] + 0.5 * gbuf[f]

    loop(1, 7, lambda i: prim_plane(mid, q2, i))
    loop(1, 6, lambda i: face_plane(mid, q2, i))
    loop(2, 6, lambda i: update_plane(mid, q2, i, fnew, i - 2))
    store_fine = pltpu.make_async_copy(fnew, fine_out.at[0], in_sem.at[0])
    store_fine.start()

    def put(k, value):
        for h in range(2):
            sums[k, h] = value[:, 128 * h : 128 * (h + 1)]

    for f in range(F):
        put(3 * f + 2, scale * (face_sum[f] + fx[f, edge]))
        for r in range(2):
            put(3 * f + r, 0.125 * (fnew[f, 2 * r] + fnew[f, 2 * r + 1]))
    rows = lax.broadcasted_iota(jnp.int32, (256, 128), 0)
    cols = lax.broadcasted_iota(jnp.int32, (256, 128), 1)
    pairs = jnp.where(lax.shift_right_logical(rows, 1) == cols, 1.0, 0.0).astype(jnp.float32)
    coarse = jnp.zeros((120, 128), jnp.float32)
    for h in range(2):
        rows_h = [
            sums[k, h, pl.ds(0, 8, stride=2), :] + sums[k, h, pl.ds(1, 8, stride=2), :]
            for k in range(15)
        ]
        coarse = coarse + jnp.dot(
            jnp.concatenate(rows_h, axis=0),
            pairs[128 * h : 128 * (h + 1)],
            precision=lax.Precision.HIGHEST,
            preferred_element_type=jnp.float32,
        )
    for f in range(F):
        for r in range(3):
            for k in range(8):
                at = (3 * f + r) * 8 + k
                rec[8 * r + k, pl.ds(f, 1), :] = coarse[at : at + 1]
    rec[24] = jnp.zeros((F, 128), jnp.float32)

    to_inv.wait()

    def fill(s, carry):
        slots[s] = rec[inv_s[0, s]]
        return carry

    lax.fori_loop(0, 64, fill, 0, unroll=8)

    for o in offsets:
        p = peer(o)
        pltpu.make_async_remote_copy(
            slots.at[p], recv.at[me], rec_s, rec_r, device_id={"grp": p}, device_id_type=MESH
        ).start()
    recv[me] = slots[me]

    def totals(buffer, send, receive):
        return pltpu.make_async_remote_copy(
            buffer.at[pl.ds(0, 63)], buffer.at[pl.ds(0, 63)], send, receive,
            device_id={"grp": peer((1, 0))}, device_id_type=MESH,
        )

    totals(code_rx, code_s, code_r).wait()
    target = (lane + 1).astype(jnp.float32)
    mine = lane == me

    def decode(s, carry):
        src, kind = carry
        value = jnp.sum(jnp.where(mine, code_rx[s], 0.0), axis=1, keepdims=True)
        average = value == target
        face = value == target + 32.0
        return (
            jnp.where(average | face, s, src),
            jnp.where(average, 1, jnp.where(face, 2, kind)),
        )

    zero = jnp.zeros((1, 128), jnp.int32)
    src, kind = lax.fori_loop(0, 64, decode, (zero, zero), unroll=8)
    idx_v[0] = src
    idx_v[1] = kind
    to_src = pltpu.make_async_copy(idx_v, src_s, in_sem.at[8])
    to_src.start()
    load_state.wait()
    load_term.wait()
    to_src.wait()

    totals(recv, rec_s, rec_r).wait()

    def combine(c, carry):
        value = recv[src_s[0, 0, c]]
        kind = src_s[1, 0, c]
        base = state_v[c]
        coarse_v[c] = jnp.where(
            kind == 1, value, jnp.where(kind == 2, base + value - term_v[c], base)
        )
        return carry

    lax.fori_loop(0, 24, combine, 0, unroll=8)
    store_coarse = pltpu.make_async_copy(coarse_v, coarse_out.at[0, 0], in_sem.at[1])
    store_coarse.start()
    store_fine.wait()
    store_coarse.wait()


def on_device(fine_state, patch_ghosts, coarse_state, coarse_face_term, dest_grp, dest_column):
    any_spec = pl.BlockSpec(memory_space=pl.ANY)
    vm, f32 = pltpu.VMEM, jnp.float32
    dma = pltpu.SemaphoreType.DMA
    return pl.pallas_call(
        kernel,
        out_shape=(
            jax.ShapeDtypeStruct(fine_state.shape, f32),
            jax.ShapeDtypeStruct(coarse_state.shape, f32),
        ),
        in_specs=[any_spec] * 6,
        out_specs=(any_spec, any_spec),
        scratch_shapes=[
            vm((F, 8, 16, 256), f32),
            vm((F, 8, 16, 256), f32),
            vm((F, 8, 16, 256), f32),
            vm((F, 8, 16, 256), f32),
            vm((F, 8, 16, 256), f32),
            vm((F, 4, 16, 256), f32),
            vm((F, 16, 256), f32),
            vm((F, 16, 256), f32),
            vm((15, 2, 16, 128), f32),
            vm((25, F, 128), f32),
            vm((64, F, 128), f32),
            vm((64, F, 128), f32),
            vm((1, 128), f32),
            vm((64, 1, 128), f32),
            vm((2, 1, 128), jnp.int32),
            vm((24, F, 128), f32),
            vm((24, F, 128), f32),
            vm((24, F, 128), f32),
            pltpu.SMEM((1, 1, 24), jnp.int32),
            pltpu.SMEM((1, 1, 24), jnp.int32),
            pltpu.SMEM((1, 128), jnp.int32),
            pltpu.SMEM((2, 1, 128), jnp.int32),
            dma((9,)),
            dma((2,)),
            dma((2,)),
            dma,
            dma,
            dma,
            dma,
        ],
        compiler_params=pltpu.CompilerParams(collective_id=0, has_side_effects=True),
    )(fine_state, patch_ghosts, coarse_state, coarse_face_term, dest_grp, dest_column)


def solution(mesh):
    in_specs = (
        P("grp", None, "box", None, None),
        P("grp", None, None, None, None, None),
        P("grp", "box", None, None, None),
        P("grp", "box", None, None, None),
        P("grp", "box", None),
        P("grp", "box", None),
    )
    out_specs = (P("grp", None, "box", None, None), P("grp", "box", None, None, None))
    return jax.shard_map(
        on_device, mesh=mesh, in_specs=in_specs, out_specs=out_specs, check_vma=False
    )
```

time: 81 us -> 39.8 us (0.49)
  the two profiles are of different devices: /device:TPU:1 before, /device:TPU:17 now
where the time goes in v1:
time: 39.8 us; the launch traced here: 39.6 us
  Pallas kernels  33.5 us (84%)
  local copies, waits for them, and re-layouts  5.42 us (14%)
  between operations  0.65 us (2%)
    pallas_call x1, Pallas kernels, on_device(): pl.pallas_call(kernel, out_shape=(jax.ShapeDtypeStruct(fine_state.shape,...  33.5 us
    unnamed x5, local copies, waits for them, and re-layouts  3.89 us
    pallas_call x1, local copies, waits for them, and re-layouts, on_device(): pl.pallas_call(kernel, out_shape=(jax.ShapeDtypeStruct(fine_state.shape,...  1.53 us

profile of v1, /device:TPU:17, one launch (start us, length us, event | category | flops | bytes accessed | tf_op | source)
XLA Modules:
  0.0 39.6 jit_solution(1809415583312956230)
XLA Ops:
  0.6 0.0 copy-start
  0.6 1.5 %copy.8.state = f32[1,1,24,5,128]{4,3,2,1,0:T(8,128)} copy(f32[1,1,24,5,128]{4,2,3,1,0:T(8,128)} %param.8) | data formatting | bytes 122880 | tf_op args[2]
  2.1 0.0 copy-done
  2.1 0.7 %copy.9.term = f32[1,1,24,5,128]{4,3,2,1,0:T(8,128)} copy(f32[1,1,24,5,128]{4,2,3,1,0:T(8,128)S(1)} %copy-done) | data formatting | bytes 122880 | tf_op args[3]
  2.8 33.5 %shard_map.77 = (f32[1,5,4,16,256]{4,3,2,1,0:T(8,128)}, f32[1,1,24,5,128]{4,3,2,1,0:T(8,128)}) custom-call(f32[1,5,4,16,256]{4,3,2,1,0:T(8,128)} %fine.1, f32[1,2,2,5,16,256]{5,4,3,2,1,0:T(8,128)} %ghosts.1, f32[1,1,24,5,128]{4,3,2,1,0:T(8,128)} %copy.8.state, f32[1,1,24,5,128]{4,3,2,1,0:T(8,128)} %copy.9.term, s32[1,1,24]{2,1,0:T(1,128)} %dgrp.1, ...), custom_call_target="tpu_custom_call" | custom-call | tf_op jit(solution)/shard_map/pallas_call | solution.py:332
  36.3 1.5 %copy.10 = f32[1,1,24,5,128]{4,2,3,1,0:T(8,128)} copy(f32[1,1,24,5,128]{4,3,2,1,0:T(8,128)} %get-tuple-element.3) | data formatting | bytes 122880 | tf_op jit(solution)/shard_map/pallas_call | solution.py:332
  37.8 1.7 %copy.12 = f32[1,5,4,16,256]{4,3,2,1,0:T(8,128)} copy(f32[1,5,4,16,256]{4,3,2,1,0:T(8,128)} %get-tuple-element.6) | data formatting | bytes 655360
Async XLA Ops:
  0.6 1.5 %copy-start = (f32[1,1,24,5,128]{4,2,3,1,0:T(8,128)S(1)}, f32[1,1,24,5,128]{4,2,3,1,0:T(8,128)}, u32[]{:S(2)}) copy-start(f32[1,1,24,5,128]{4,2,3,1,0:T(8,128)} %param.9) | copy-start | bytes 184324

commit v2 on v1

v2 whole, which is shorter than its diff:
```python
import jax
import jax.numpy as jnp
from jax import lax
from jax.experimental import pallas as pl
from jax.experimental.pallas import tpu as pltpu
from jax.sharding import PartitionSpec as P

MESH = pl.DeviceIdType.MESH
HALF_STEP = 0.03
NX, NZ, NB = 4, 16, 8
F, REC, NAVG, CZ = 5, 24, 16, 128


def primitives(u):
    inverse = 1.0 / u[0]
    v = [u[1] * inverse, u[2] * inverse, u[3] * inverse]
    kinetic = 0.5 * (u[1] * v[0] + u[2] * v[1] + u[3] * v[2])
    pressure = 0.4 * (u[4] - kinetic)
    sound = jnp.sqrt(1.4 * pressure * inverse)
    return v + [pressure, sound]


def flux(u, q, d):
    out = [u[1 + d]]
    for m in range(3):
        f = u[1 + m] * q[d]
        out.append(f + q[3] if m == d else f)
    out.append((u[4] + q[3]) * q[d])
    return out


def kernel(
    fine, ghosts, state, term, dgrp, dcol,
    fnew, coarse_out,
    ext, mid, q1, q2, fx, gbuf, face_sum, sums, rec, slots, recv, gathered,
    code_tx, code_x, bundle, code_z, table, found, state_v, term_v,
    dg_s, dc_s, inv_s, src_s,
    in_sem, halo_s, halo_r, cx_s, cx_r, cz_s, cz_r, rec_s, rec_r, hello,
):
    me = lax.axis_index("grp")
    box = lax.axis_index("box")
    at_low = box == 0
    at_high = box == NB - 1
    mx, mz = lax.div(me, NZ), lax.rem(me, NZ)

    def peer(dx, dz):
        return lax.rem(mx + dx, NX) * NZ + lax.rem(mz + dz, NZ)

    def signal(sem, **where):
        pl.semaphore_signal(sem, inc=1, device_id=where, device_id_type=MESH)

    def greet(sem, steps):
        for dx, dz in steps:
            signal(sem, grp=peer(dx, dz))

    barrier = pltpu.get_barrier_semaphore()

    @pl.when(jnp.logical_not(at_low))
    def _():
        signal(barrier, box=box - 1)

    @pl.when(jnp.logical_not(at_high))
    def _():
        signal(barrier, box=box + 1)

    rows = [(dx, 0) for dx in range(1, NX)]
    greet(barrier, [(0, 1), (0, NZ - 1)] + rows)

    def local(src, dst, at):
        return pltpu.make_async_copy(src, dst, in_sem.at[at])

    load_fine = local(fine.at[0], ext.at[:, pl.ds(2, 4)], 0)
    load_dg = local(dgrp, dg_s, 1)
    load_dc = local(dcol, dc_s, 2)
    load_state = local(state, state_v, 3)
    load_term = local(term, term_v, 4)
    load_fine.start()
    load_dg.start()
    load_dc.start()

    def ghost_loads(side):
        near, far = (1, 0) if side == 0 else (6, 7)
        return [
            local(ghosts.at[0, 0, side], ext.at[:, near], 5),
            local(ghosts.at[0, 0, side], ext.at[:, far], 6),
            local(ghosts.at[0, 1, side], gbuf, 7),
        ]

    @pl.when(at_low)
    def _():
        for c in ghost_loads(0):
            c.start()

    @pl.when(at_high)
    def _():
        for c in ghost_loads(1):
            c.start()

    load_state.start()
    load_term.start()

    lane = lax.broadcasted_iota(jnp.int32, (1, 128), 1)
    load_dg.wait()
    load_dc.wait()
    live_face = jnp.where(at_low | at_high, 1, 0)
    which = jnp.full((1, 128), REC, jnp.int32)
    code = jnp.zeros((1, 128), jnp.int32)
    for r in range(REC):
        hit = lane == dg_s[0, 0, r]
        which = jnp.where(hit, r, which)
        value = dc_s[0, 0, r] + 1
        if r >= NAVG:
            value = (value + 32) * live_face
        code = jnp.where(hit, value, code)
    code_tx[...] = code.astype(jnp.float32)
    table[...] = which
    to_inv = local(table, inv_s, 8)
    to_inv.start()

    load_fine.wait()
    pl.semaphore_wait(barrier, NX + 1 + jnp.where(at_low | at_high, 1, 2))

    def halo_down():
        return pltpu.make_async_remote_copy(
            ext.at[:, pl.ds(2, 2)], ext.at[:, pl.ds(6, 2)], halo_s.at[0], halo_r.at[0],
            device_id={"box": box - 1}, device_id_type=MESH,
        )

    def halo_up():
        return pltpu.make_async_remote_copy(
            ext.at[:, pl.ds(4, 2)], ext.at[:, pl.ds(0, 2)], halo_s.at[1], halo_r.at[1],
            device_id={"box": box + 1}, device_id_type=MESH,
        )

    @pl.when(jnp.logical_not(at_low))
    def _():
        halo_down().start()

    @pl.when(jnp.logical_not(at_high))
    def _():
        halo_up().start()

    greet(hello.at[0], [(0, 1), (0, NZ - 1)])

    def send(src, dst, s, r, to):
        return pltpu.make_async_remote_copy(
            src, dst, s, r, device_id={"grp": to}, device_id_type=MESH
        )

    for dx in range(1, NX):
        send(code_tx, code_x.at[mx], cx_s, cx_r, peer(dx, 0)).start()
    code_x[mx] = code_tx[...]

    def prim_plane(u_ref, q_ref, i):
        q = primitives([u_ref[f, i] for f in range(F)])
        for f in range(F):
            q_ref[f, i] = q[f]

    def face_plane(u_ref, q_ref, i):
        ul, ur = [u_ref[f, i] for f in range(F)], [u_ref[f, i + 1] for f in range(F)]
        ql, qr = [q_ref[f, i] for f in range(F)], [q_ref[f, i + 1] for f in range(F)]
        fl, fr = flux(ul, ql, 0), flux(ur, qr, 0)
        biggest = jnp.maximum(jnp.abs(ql[0]) + ql[4], jnp.abs(qr[0]) + qr[4])
        for f in range(F):
            fx[f, i] = (fl[f] + fr[f]) - biggest * (ur[f] - ul[f])

    def update_plane(u_ref, q_ref, i, dst, j):
        u = [u_ref[f, i] for f in range(F)]
        q = [q_ref[f, i] for f in range(F)]
        change = [fx[f, i] - fx[f, i - 1] for f in range(F)]
        for d, axis, size in ((1, 0, 16), (2, 1, 256)):
            fl = flux(u, q, d)
            s = jnp.abs(q[d]) + q[4]
            biggest = jnp.maximum(s, pltpu.roll(s, size - 1, axis))
            for f in range(F):
                up, fp = pltpu.roll(u[f], size - 1, axis), pltpu.roll(fl[f], size - 1, axis)
                face = (fl[f] + fp) - biggest * (up - u[f])
                change[f] = change[f] + (face - pltpu.roll(face, 1, axis))
        for f in range(F):
            dst[f, j] = u[f] - HALF_STEP * change[f]

    def loop(start, count, body):
        def step(i, carry):
            body(start + i)
            return carry

        lax.fori_loop(0, count, step, 0)

    loop(2, 4, lambda i: prim_plane(ext, q1, i))
    pl.semaphore_wait(hello.at[0], 2)
    greet(hello.at[1], [(0, 2), (0, NZ - 2)])
    loop(2, 3, lambda i: face_plane(ext, q1, i))
    loop(3, 2, lambda i: update_plane(ext, q1, i, mid, i))

    def row_total(buffer, count, s, r):
        return send(buffer.at[pl.ds(0, count)], buffer.at[pl.ds(0, count)], s, r, peer(0, 1))

    row_total(code_x, NX - 1, cx_s, cx_r).wait()
    packed = jnp.zeros((1, 128), jnp.float32)
    for sx in range(NX):
        moved = pltpu.roll(code_x[sx], lax.rem(128 + (sx - mx) * NZ, 128), 1)
        packed = jnp.where((lane >= sx * NZ) & (lane < (sx + 1) * NZ), moved, packed)
    bundle[...] = packed
    code_z[mz] = packed

    def side(low):
        p, e, u = (jnp.where(low, 0, 6), jnp.where(low, 0, 5), jnp.where(low, 1, 5))
        loop(p, 2, lambda i: prim_plane(ext, q1, i))
        loop(e, 2, lambda i: face_plane(ext, q1, i))
        loop(u, 2, lambda i: update_plane(ext, q1, i, mid, i))

    def wait_low():
        @pl.when(jnp.logical_not(at_low))
        def _():
            halo_down().wait_send()
            halo_up().wait_recv()

        @pl.when(at_low)
        def _():
            for c in ghost_loads(0):
                c.wait()

    def wait_high():
        @pl.when(jnp.logical_not(at_high))
        def _():
            halo_up().wait_send()
            halo_down().wait_recv()

        @pl.when(at_high)
        def _():
            for c in ghost_loads(1):
                c.wait()

    odd = lax.rem(box, 2) == 1
    even = jnp.logical_not(odd)

    @pl.when(odd)
    def _():
        wait_low()

    @pl.when(even)
    def _():
        wait_high()

    side(odd)
    pl.semaphore_wait(hello.at[1], 2)
    greet(hello.at[2], [(0, 4), (0, NZ - 4)])

    @pl.when(odd)
    def _():
        wait_high()

    @pl.when(even)
    def _():
        wait_low()

    side(even)

    scale = jnp.where(at_low, -0.0075 * 0.5, 0.0075 * 0.5)
    edge = jnp.where(at_low, 1, 5)
    for f in range(F):
        face_sum[f] = fx[f, edge]

    @pl.when(at_low)
    def _():
        for f in range(F):
            mid[f, 1] = 0.5 * ext[f, 1] + 0.5 * gbuf[f]

    @pl.when(at_high)
    def _():
        for f in range(F):
            mid[f, 6] = 0.5 * ext[f, 6] + 0.5 * gbuf[f]

    loop(1, 6, lambda i: prim_plane(mid, q2, i))
    loop(1, 5, lambda i: face_plane(mid, q2, i))
    loop(2, 4, lambda i: update_plane(mid, q2, i, fnew, i - 2))

    def put(k, value):
        for h in range(2):
            sums[k, h] = value[:, 128 * h : 128 * (h + 1)]

    for f in range(F):
        put(3 * f + 2, scale * (face_sum[f] + fx[f, edge]))
        for r in range(2):
            put(3 * f + r, 0.125 * (fnew[f, 2 * r] + fnew[f, 2 * r + 1]))
    fine_z = lax.broadcasted_iota(jnp.int32, (256, CZ), 0)
    coarse_z = lax.broadcasted_iota(jnp.int32, (256, CZ), 1)
    pairs = jnp.where(lax.shift_right_logical(fine_z, 1) == coarse_z, 1.0, 0.0).astype(jnp.float32)
    coarse = jnp.zeros((3 * F * 8, CZ), jnp.float32)
    for h in range(2):
        part = [
            sums[k, h, pl.ds(0, 8, stride=2), :] + sums[k, h, pl.ds(1, 8, stride=2), :]
            for k in range(3 * F)
        ]
        coarse = coarse + jnp.dot(
            jnp.concatenate(part, axis=0),
            pairs[128 * h : 128 * (h + 1)],
            precision=lax.Precision.HIGHEST,
            preferred_element_type=jnp.float32,
        )
    for f in range(F):
        for r in range(3):
            for k in range(8):
                at = (3 * f + r) * 8 + k
                rec[8 * r + k, pl.ds(f, 1), :] = coarse[at : at + 1]
    rec[REC] = jnp.zeros((F, CZ), jnp.float32)

    pl.semaphore_wait(hello.at[2], 2)
    greet(hello.at[3], rows)
    to_inv.wait()

    def fill(s, carry):
        slots[s] = rec[jnp.clip(inv_s[0, s], 0, REC)]
        return carry

    lax.fori_loop(0, NX * NZ, fill, 0, unroll=8)

    def send_rows(steps):
        for dz in steps:
            for dx in (2, 1, 3, 0):
                if (dx, dz) != (0, 0):
                    to = peer(dx, dz)
                    send(slots.at[to], recv.at[me], rec_s, rec_r, to).start()

    def send_codes(steps):
        for dz in steps:
            send(bundle, code_z.at[mz], cz_s, cz_r, peer(0, dz)).start()

    send_rows([7, 9, 6, 10])
    pl.semaphore_wait(hello.at[3], NX - 1)
    send_rows([8])
    send_codes([8, 7, 9, 6, 10, 5, 11, 4, 12, 3, 13, 2, 14, 1, 15])
    send_rows([5, 11, 4, 12, 3, 13, 2, 14, 1, 15, 0])
    recv[me] = slots[me]
    recv[NX * NZ] = jnp.zeros((F, CZ), jnp.float32)

    row_total(code_z, NZ - 1, cz_s, cz_r).wait()
    owner_z = lax.bitwise_and(lane, NZ - 1) == mz
    valid = owner_z & (lane < NX * NZ)
    source = lax.bitwise_and(lane, -NZ) + 1
    hits = []
    for c in range(REC):
        hits.append(jnp.zeros((1, 128), jnp.int32))
    for sz in range(NZ):
        codes = jnp.where(valid, code_z[sz].astype(jnp.int32), 0)
        slot = source + sz
        for c in range(REC):
            average, face = codes == c + 1, codes == c + 33
            hits[c] = hits[c] + jnp.where(average, slot, jnp.where(face, slot + 128, 0))
    total = jnp.sum(
        jnp.concatenate(hits, axis=0).astype(jnp.float32), axis=1, keepdims=True
    ).astype(jnp.int32)
    total = jnp.broadcast_to(total, (REC, 128))
    is_face = total > 128
    found[...] = jnp.where(total == 0, NX * NZ, jnp.where(is_face, total - 129, total - 1))
    to_src = local(found, src_s, 8)
    to_src.start()
    load_state.wait()
    load_term.wait()
    for f in range(F):
        base = state_v[f]
        state_v[f] = jnp.where(
            total == 0, base, jnp.where(is_face, base - term_v[f], jnp.zeros_like(base))
        )
    to_src.wait()

    row_total(recv, NX * NZ - 1, rec_s, rec_r).wait()
    for c in range(REC):
        value = recv[jnp.clip(src_s[c, 0], 0, NX * NZ)]
        for f in range(F):
            gathered[f, pl.ds(c, 1), :] = value[f : f + 1]
    for f in range(F):
        coarse_out[f] = state_v[f] + gathered[f]


def store_kernel(fine_v, coarse_v, fine_out, coarse_out, sem):
    copies = [
        pltpu.make_async_copy(fine_v, fine_out.at[0], sem.at[0]),
        pltpu.make_async_copy(coarse_v, coarse_out, sem.at[1]),
    ]
    for c in copies:
        c.start()
    for c in copies:
        c.wait()


def on_device(fine_state, patch_ghosts, coarse_state, coarse_face_term, dest_grp, dest_column):
    any_spec = pl.BlockSpec(memory_space=pl.ANY)
    vmem_spec = pl.BlockSpec(memory_space=pltpu.VMEM)
    vm, sm, f32, i32 = pltpu.VMEM, pltpu.SMEM, jnp.float32, jnp.int32
    dma = pltpu.SemaphoreType.DMA
    fine_new, coarse_new = pl.pallas_call(
        kernel,
        out_shape=(vm((F, 4, 16, 256), f32), vm((F, REC, CZ), f32)),
        in_specs=[any_spec] * 6,
        out_specs=(vmem_spec, vmem_spec),
        scratch_shapes=[
            vm((F, 8, 16, 256), f32),
            vm((F, 8, 16, 256), f32),
            vm((F, 8, 16, 256), f32),
            vm((F, 8, 16, 256), f32),
            vm((F, 8, 16, 256), f32),
            vm((F, 16, 256), f32),
            vm((F, 16, 256), f32),
            vm((3 * F, 2, 16, 128), f32),
            vm((REC + 1, F, CZ), f32),
            vm((NX * NZ, F, CZ), f32),
            vm((NX * NZ + 1, F, CZ), f32),
            vm((F, REC, CZ), f32),
            vm((1, 128), f32),
            vm((NX, 1, 128), f32),
            vm((1, 128), f32),
            vm((NZ, 1, 128), f32),
            vm((1, 128), i32),
            vm((REC, 128), i32),
            vm((F, REC, CZ), f32),
            vm((F, REC, CZ), f32),
            sm((1, 1, REC), i32),
            sm((1, 1, REC), i32),
            sm((1, 128), i32),
            sm((REC, 128), i32),
            dma((9,)),
            dma((2,)),
            dma((2,)),
            dma,
            dma,
            dma,
            dma,
            dma,
            dma,
            pltpu.SemaphoreType.REGULAR((4,)),
        ],
        compiler_params=pltpu.CompilerParams(collective_id=0, has_side_effects=True),
    )(
        fine_state,
        patch_ghosts,
        coarse_state[0, 0].transpose(1, 0, 2),
        coarse_face_term[0, 0].transpose(1, 0, 2),
        dest_grp,
        dest_column,
    )
    fine_new, coarse_new = pl.pallas_call(
        store_kernel,
        out_shape=(
            jax.ShapeDtypeStruct(fine_state.shape, f32),
            jax.ShapeDtypeStruct((F, REC, CZ), f32),
        ),
        in_specs=[vmem_spec] * 2,
        out_specs=(any_spec, any_spec),
        scratch_shapes=[dma((2,))],
    )(
        pltpu.with_memory_space_constraint(fine_new, vm),
        pltpu.with_memory_space_constraint(coarse_new, vm),
    )
    return fine_new, coarse_new.transpose(1, 0, 2)[None, None]


def solution(mesh):
    in_specs = (
        P("grp", None, "box", None, None),
        P("grp", None, None, None, None, None),
        P("grp", "box", None, None, None),
        P("grp", "box", None, None, None),
        P("grp", "box", None),
        P("grp", "box", None),
    )
    out_specs = (P("grp", None, "box", None, None), P("grp", "box", None, None, None))
    return jax.shard_map(
        on_device, mesh=mesh, in_specs=in_specs, out_specs=out_specs, check_vma=False
    )
```

time: 39.8 us -> 32.4 us (0.81)
  the two profiles are of different devices: /device:TPU:17 before, /device:TPU:8 now
where the time goes in v2:
time: 32.4 us; the launch traced here: 32.3 us
  Pallas kernels  31.7 us (98%)
  between operations  0.64 us (2%)
    pallas_call x1, Pallas kernels, on_device(): pl.pallas_call(kernel, out_shape=(vm((F, 4, 16, 256), f32), vm((F, REC, C...  30.9 us
    pallas_call x1, Pallas kernels, on_device(): pl.pallas_call(store_kernel, out_shape=(jax.ShapeDtypeStruct(fine_state.s...  0.75 us

profile of v2, /device:TPU:8, one launch (start us, length us, event | category | flops | bytes accessed | tf_op | source)
XLA Modules:
  0.0 32.3 jit_solution(13928421463966469597)
XLA Ops:
  0.6 30.9 %shard_map.77 = (f32[5,4,16,256]{3,2,1,0:T(8,128)S(1)}, f32[5,24,128]{2,1,0:T(8,128)S(1)}) custom-call(f32[1,5,4,16,256]{4,3,2,1,0:T(8,128)} %fine.1, f32[1,2,2,5,16,256]{5,4,3,2,1,0:T(8,128)} %ghosts.1, f32[5,24,128]{2,1,0:T(8,128)} %bitcast.9, f32[5,24,128]{2,1,0:T(8,128)} %bitcast.10, s32[1,1,24]{2,1,0:T(1,128)} %dgrp.1, s32[1,1,24]{2,1,0:T(1,128)} %dcol.1), custom_call_target="tpu_custom_call" | custom-call | tf_op jit(solution)/shard_map/pallas_call | solution.py:392
  31.5 0.8 %shard_map.78 = (f32[1,5,4,16,256]{4,3,2,1,0:T(8,128)}, f32[5,24,128]{2,1,0:T(8,128)}) custom-call(f32[5,4,16,256]{3,2,1,0:T(8,128)S(1)} %get-tuple-element.6.fine_v, f32[5,24,128]{2,1,0:T(8,128)S(1)} %get-tuple-element.7.coarse_v), custom_call_target="tpu_custom_call" | custom-call | tf_op jit(solution)/shard_map/pallas_call | solution.py:442

commit v3 on v2

v3 whole, which is shorter than its diff:
```python
import jax
import jax.numpy as jnp
from jax import lax
from jax.experimental import pallas as pl
from jax.experimental.pallas import tpu as pltpu
from jax.sharding import PartitionSpec as P

MESH = pl.DeviceIdType.MESH
HALF_STEP = 0.03
NX, NZ, NB = 4, 16, 8
F, REC, NAVG, CZ = 5, 24, 16, 128


def primitives(u):
    inverse = 1.0 / u[0]
    v = [u[1] * inverse, u[2] * inverse, u[3] * inverse]
    kinetic = 0.5 * (u[1] * v[0] + u[2] * v[1] + u[3] * v[2])
    pressure = 0.4 * (u[4] - kinetic)
    sound = jnp.sqrt(1.4 * pressure * inverse)
    return v + [pressure, sound]


def flux(u, q, d):
    out = [u[1 + d]]
    for m in range(3):
        f = u[1 + m] * q[d]
        out.append(f + q[3] if m == d else f)
    out.append((u[4] + q[3]) * q[d])
    return out


def face(ul, ur, fl, fr, sl, sr):
    biggest = jnp.maximum(sl, sr)
    return [(fl[f] + fr[f]) - biggest * (ur[f] - ul[f]) for f in range(F)]


def exact_dot(x, to):
    total = None
    for _ in range(3):
        part = x.astype(jnp.bfloat16)
        x = x - part.astype(jnp.float32)
        moved = jnp.dot(part, to, preferred_element_type=jnp.float32)
        total = moved if total is None else total + moved
    return total


def turned(a, axis, shift):
    return pltpu.roll(a, shift % (8, 128)[axis], axis)


def kernel(
    fine, ghosts, state, term, dgrp, dcol,
    fine_out, coarse_out,
    raw, graw, ext, mid, q1, q2, fx, fnew, gbuf, face_sum, rec, slots, recv, gathered,
    code_tx, code_x, bundle, code_z, table, found, state_v, term_v,
    dg_s, dc_s, inv_s, src_s,
    in_sem, halo_s, halo_r, cx_s, cx_r, cz_s, cz_r, rec_s, rec_r, hello,
):
    me = lax.axis_index("grp")
    box = lax.axis_index("box")
    at_low = box == 0
    at_high = box == NB - 1
    mx, mz = lax.div(me, NZ), lax.rem(me, NZ)

    def peer(dx, dz):
        return lax.rem(mx + dx, NX) * NZ + lax.rem(mz + dz, NZ)

    def signal(sem, **where):
        pl.semaphore_signal(sem, inc=1, device_id=where, device_id_type=MESH)

    def greet(sem, steps):
        for dz in steps:
            signal(sem, grp=peer(0, dz))
            signal(sem, grp=peer(0, NZ - dz))

    barrier = pltpu.get_barrier_semaphore()

    @pl.when(jnp.logical_not(at_low))
    def _():
        signal(barrier, box=box - 1)

    @pl.when(jnp.logical_not(at_high))
    def _():
        signal(barrier, box=box + 1)

    greet(barrier, [1, 2])
    for dx in range(1, NX):
        signal(barrier, grp=peer(dx, 0))

    def local(src, dst, at):
        return pltpu.make_async_copy(src, dst, in_sem.at[at])

    def halves(src, dst, at):
        return [
            local(src.at[:, :, pl.ds(128 * h, 128)], dst.at[:, h], at + h) for h in (0, 1)
        ]

    load_fine = [
        local(fine.at[0, :, :, :, pl.ds(128 * h, 128)], raw.at[:, :, h], h) for h in (0, 1)
    ]
    load_dg = local(dgrp, dg_s, 2)
    load_dc = local(dcol, dc_s, 3)
    load_state = local(state, state_v, 4)
    load_term = local(term, term_v, 5)
    for c in load_fine:
        c.start()
    load_dg.start()
    load_dc.start()

    def ghost_loads(end):
        return [c for t in (0, 1) for c in halves(ghosts.at[0, t, end], graw.at[t], 6 + 2 * t)]

    @pl.when(at_low)
    def _():
        for c in ghost_loads(0):
            c.start()

    @pl.when(at_high)
    def _():
        for c in ghost_loads(1):
            c.start()

    load_state.start()
    load_term.start()

    lane = lax.broadcasted_iota(jnp.int32, (1, 128), 1)
    load_dg.wait()
    load_dc.wait()
    live_face = jnp.where(at_low | at_high, 1, 0)
    which = jnp.full((1, 128), REC, jnp.int32)
    code = jnp.zeros((1, 128), jnp.int32)
    for r in range(REC):
        hit = lane == dg_s[0, 0, r]
        which = jnp.where(hit, r, which)
        value = dc_s[0, 0, r] + 1
        if r >= NAVG:
            value = (value + 32) * live_face
        code = jnp.where(hit, value, code)
    code_tx[...] = code.astype(jnp.float32)
    table[...] = which
    to_inv = local(table, inv_s, 10)
    to_inv.start()

    row = lax.broadcasted_iota(jnp.int32, (256, 256), 0)
    col = lax.broadcasted_iota(jnp.int32, (256, 256), 1)

    def cell(split):
        return 2 * lax.bitwise_and(split, 127) + lax.shift_right_logical(split, 7)

    to_split = jnp.where(row == cell(col), 1.0, 0.0).astype(jnp.bfloat16)

    def split_plane(lines, put):
        moved = exact_dot(jnp.concatenate(lines, axis=0), to_split)
        for f in range(F):
            for py in (0, 1):
                at = 8 * (2 * f + py)
                for pz in (0, 1):
                    put(f, 2 * py + pz, moved[at : at + 8, 128 * pz : 128 * (pz + 1)])

    def loop(start, count, body, unroll=1):
        def step(i, carry):
            body(start + i)
            return carry

        lax.fori_loop(0, count, step, 0, unroll=unroll)

    for c in load_fine:
        c.wait()

    def split_fine(i):
        lines = [
            jnp.concatenate([raw[f, i, h, pl.ds(py, 8, stride=2), :] for h in (0, 1)], axis=1)
            for f in range(F)
            for py in (0, 1)
        ]

        def put(f, k, value):
            ext[f, i + 2, k] = value

        split_plane(lines, put)

    loop(0, 4, split_fine, 4)

    pl.semaphore_wait(barrier, NX + 3 + jnp.where(at_low | at_high, 1, 2))

    def halo_down():
        return pltpu.make_async_remote_copy(
            ext.at[:, pl.ds(2, 2)], ext.at[:, pl.ds(6, 2)], halo_s.at[0], halo_r.at[0],
            device_id={"box": box - 1}, device_id_type=MESH,
        )

    def halo_up():
        return pltpu.make_async_remote_copy(
            ext.at[:, pl.ds(4, 2)], ext.at[:, pl.ds(0, 2)], halo_s.at[1], halo_r.at[1],
            device_id={"box": box + 1}, device_id_type=MESH,
        )

    @pl.when(jnp.logical_not(at_low))
    def _():
        halo_down().start()

    @pl.when(jnp.logical_not(at_high))
    def _():
        halo_up().start()

    greet(hello.at[0], [1, 2])

    def send(src, dst, s, r, to):
        return pltpu.make_async_remote_copy(
            src, dst, s, r, device_id={"grp": to}, device_id_type=MESH
        )

    for dx in range(1, NX):
        send(code_tx, code_x.at[mx], cx_s, cx_r, peer(dx, 0)).start()
    code_x[mx] = code_tx[...]

    def prim_plane(u_ref, q_ref, i):
        for k in range(4):
            q = primitives([u_ref[f, i, k] for f in range(F)])
            for f in range(F):
                q_ref[f, i, k] = q[f]

    def sides(u_ref, q_ref, places, d):
        out = []
        for i, k in places:
            u, q = [[ref[f, i, k] for f in range(F)] for ref in (u_ref, q_ref)]
            out.append((u, flux(u, q, d), jnp.abs(q[d]) + q[4]))
        return out

    def face_plane(u_ref, q_ref, i):
        for k in range(4):
            (ul, fl, sl), (ur, fr, sr) = sides(u_ref, q_ref, ((i, k), (i + 1, k)), 0)
            for f, value in enumerate(face(ul, ur, fl, fr, sl, sr)):
                fx[f, i, k] = value

    def update_plane(u_ref, q_ref, i, dst, j):
        change = [[fx[f, i, k] - fx[f, i - 1, k] for k in range(4)] for f in range(F)]
        for d, pairs in ((1, ((0, 2), (1, 3))), (2, ((0, 1), (2, 3)))):
            for even, odd in pairs:
                (ue, fe, se), (uo, fo, so) = sides(u_ref, q_ref, ((i, even), (i, odd)), d)
                inner = face(ue, uo, fe, fo, se, so)
                un, fn = [[turned(a, d - 1, -1) for a in part] for part in (ue, fe)]
                outer = face(uo, un, fo, fn, so, turned(se, d - 1, -1))
                for f in range(F):
                    change[f][even] = change[f][even] + (inner[f] - turned(outer[f], d - 1, 1))
                    change[f][odd] = change[f][odd] + (outer[f] - inner[f])
        for f in range(F):
            for k in range(4):
                dst[f, j, k] = u_ref[f, i, k] - HALF_STEP * change[f][k]

    loop(2, 4, lambda i: prim_plane(ext, q1, i), 2)
    loop(2, 3, lambda i: face_plane(ext, q1, i))
    pl.semaphore_wait(hello.at[0], 4)
    greet(hello.at[1], [4])
    loop(3, 2, lambda i: update_plane(ext, q1, i, mid, i), 2)

    def row_total(buffer, count, s, r):
        return send(buffer.at[pl.ds(0, count)], buffer.at[pl.ds(0, count)], s, r, peer(0, 1))

    row_total(code_x, NX - 1, cx_s, cx_r).wait()
    packed = jnp.zeros((1, 128), jnp.float32)
    for sx in range(NX):
        moved = pltpu.roll(code_x[sx], lax.rem(128 + (sx - mx) * NZ, 128), 1)
        packed = jnp.where((lane >= sx * NZ) & (lane < (sx + 1) * NZ), moved, packed)
    bundle[...] = packed
    code_z[mz] = packed

    def side(low):
        p, e, u = (jnp.where(low, 0, 6), jnp.where(low, 0, 5), jnp.where(low, 1, 5))
        loop(p, 2, lambda i: prim_plane(ext, q1, i), 2)
        loop(e, 2, lambda i: face_plane(ext, q1, i), 2)
        loop(u, 2, lambda i: update_plane(ext, q1, i, mid, i), 2)

    def ghost_planes(end, near, far):
        for c in ghost_loads(end):
            c.wait()

        def lines(t):
            return [
                jnp.concatenate([graw[t, f, h, pl.ds(py, 8, stride=2), :] for h in (0, 1)], axis=1)
                for f in range(F)
                for py in (0, 1)
            ]

        def put_start(f, k, value):
            ext[f, near, k] = value
            ext[f, far, k] = value

        def put_middle(f, k, value):
            gbuf[f, k] = 0.5 * ext[f, near, k] + 0.5 * value

        split_plane(lines(0), put_start)
        split_plane(lines(1), put_middle)

    def wait_low():
        @pl.when(jnp.logical_not(at_low))
        def _():
            halo_down().wait_send()
            halo_up().wait_recv()

        @pl.when(at_low)
        def _():
            ghost_planes(0, 1, 0)

    def wait_high():
        @pl.when(jnp.logical_not(at_high))
        def _():
            halo_up().wait_send()
            halo_down().wait_recv()

        @pl.when(at_high)
        def _():
            ghost_planes(1, 6, 7)

    odd = lax.rem(box, 2) == 1
    even = jnp.logical_not(odd)

    @pl.when(odd)
    def _():
        wait_low()

    @pl.when(even)
    def _():
        wait_high()

    side(odd)

    def second(prim, faces, update):
        loop(prim[0], prim[1], lambda i: prim_plane(mid, q2, i), 2)
        loop(faces[0], faces[1], lambda i: face_plane(mid, q2, i))
        loop(update, 2, lambda i: update_plane(mid, q2, i, fnew, i - 2), 2)

    first = jnp.where(odd, 1, 3)
    second((first, 4), (first, 3), first + 1)

    @pl.when(odd)
    def _():
        wait_high()

    @pl.when(even)
    def _():
        wait_low()

    side(even)

    scale = jnp.where(at_low, -0.0075 * 0.5, 0.0075 * 0.5)
    edge = jnp.where(at_low, 1, 5)
    for f in range(F):
        for k in range(4):
            face_sum[f, k] = fx[f, edge, k]

    for at_end, plane in ((at_low, 1), (at_high, 6)):

        @pl.when(at_end)
        def _():
            for f in range(F):
                mid[f, plane] = gbuf[f]

    pl.semaphore_wait(hello.at[1], 2)
    for dx in range(1, NX):
        signal(hello.at[2], grp=peer(dx, 0))
    steps = [8, 7, 9, 6, 10, 5, 11, 4, 12, 3, 13, 2, 14, 1, 15]
    for dz in steps:
        send(bundle, code_z.at[mz], cz_s, cz_r, peer(0, dz)).start()

    second((jnp.where(odd, 5, 1), 2), (jnp.where(odd, 4, 1), 2), jnp.where(odd, 4, 2))

    for f in range(F):
        for r in range(3):
            if r < 2:
                parts = [fnew[f, 2 * r + x, k] for x in (0, 1) for k in range(4)]
                factor = 0.125
            else:
                parts = [face_sum[f, k] + fx[f, edge, k] for k in range(4)]
                factor = scale
            while len(parts) > 1:
                parts = [a + b for a, b in zip(parts[::2], parts[1::2])]
            rec[pl.ds(8 * r, 8), f, :] = factor * parts[0]
    rec[REC] = jnp.zeros((F, CZ), jnp.float32)

    to_inv.wait()

    def fill(s, carry):
        slots[s] = rec[jnp.clip(inv_s[0, s], 0, REC)]
        return carry

    lax.fori_loop(0, NX * NZ, fill, 0, unroll=8)

    pl.semaphore_wait(hello.at[2], NX - 1)
    for dz in steps + [0]:
        for dx in (2, 1, 3, 0):
            if (dx, dz) != (0, 0):
                to = peer(dx, dz)
                send(slots.at[to], recv.at[me], rec_s, rec_r, to).start()
    recv[me] = slots[me]
    recv[NX * NZ] = jnp.zeros((F, CZ), jnp.float32)

    to_whole = jnp.where(col == cell(row), 1.0, 0.0).astype(jnp.bfloat16)

    def whole_plane(i):
        lines = [
            jnp.concatenate([fnew[f, i, 2 * py + pz] for pz in (0, 1)], axis=1)
            for f in range(F)
            for py in (0, 1)
        ]
        moved = exact_dot(jnp.concatenate(lines, axis=0), to_whole)
        for f in range(F):
            for py in (0, 1):
                at = 8 * (2 * f + py)
                for h in (0, 1):
                    part = moved[at : at + 8, 128 * h : 128 * (h + 1)]
                    fine_out[f, i, h, pl.ds(py, 8, stride=2), :] = part

    loop(0, 4, whole_plane)

    row_total(code_z, NZ - 1, cz_s, cz_r).wait()
    owner_z = lax.bitwise_and(lane, NZ - 1) == mz
    valid = owner_z & (lane < NX * NZ)
    source = lax.bitwise_and(lane, -NZ) + 1
    hits = [jnp.zeros((1, 128), jnp.int32) for _ in range(REC)]
    for sz in range(NZ):
        codes = jnp.where(valid, code_z[sz].astype(jnp.int32), 0)
        slot = source + sz
        for c in range(REC):
            average, is_face = codes == c + 1, codes == c + 33
            hits[c] = hits[c] + jnp.where(average, slot, jnp.where(is_face, slot + 128, 0))
    total = jnp.sum(
        jnp.concatenate(hits, axis=0).astype(jnp.float32), axis=1, keepdims=True
    ).astype(jnp.int32)
    total = jnp.broadcast_to(total, (REC, 128))
    of_face = total > 128
    found[...] = jnp.where(total == 0, NX * NZ, jnp.where(of_face, total - 129, total - 1))
    to_src = local(found, src_s, 10)
    to_src.start()
    load_state.wait()
    load_term.wait()
    for f in range(F):
        base = state_v[f]
        state_v[f] = jnp.where(
            total == 0, base, jnp.where(of_face, base - term_v[f], jnp.zeros_like(base))
        )
    to_src.wait()

    row_total(recv, NX * NZ - 1, rec_s, rec_r).wait()
    for c in range(REC):
        value = recv[jnp.clip(src_s[c, 0], 0, NX * NZ)]
        gathered[pl.ds(c, F, stride=REC), :] = value
    for f in range(F):
        coarse_out[f] = state_v[f] + gathered[pl.ds(REC * f, REC), :]


def store_kernel(fine_v, coarse_v, fine_out, coarse_out, sem):
    copies = [pltpu.make_async_copy(coarse_v, coarse_out, sem.at[2])]
    for h in (0, 1):
        part = fine_out.at[0, :, :, :, pl.ds(128 * h, 128)]
        copies.append(pltpu.make_async_copy(fine_v.at[:, :, h], part, sem.at[h]))
    for c in copies:
        c.start()
    for c in copies:
        c.wait()


def on_device(fine_state, patch_ghosts, coarse_state, coarse_face_term, dest_grp, dest_column):
    any_spec = pl.BlockSpec(memory_space=pl.ANY)
    vmem_spec = pl.BlockSpec(memory_space=pltpu.VMEM)
    vm, sm, f32, i32 = pltpu.VMEM, pltpu.SMEM, jnp.float32, jnp.int32
    dma = pltpu.SemaphoreType.DMA
    fine_new, coarse_new = pl.pallas_call(
        kernel,
        out_shape=(vm((F, 4, 2, 16, 128), f32), vm((F, REC, CZ), f32)),
        in_specs=[any_spec] * 6,
        out_specs=(vmem_spec, vmem_spec),
        scratch_shapes=[
            vm((F, 4, 2, 16, 128), f32),
            vm((2, F, 2, 16, 128), f32),
            vm((F, 8, 4, 8, 128), f32),
            vm((F, 8, 4, 8, 128), f32),
            vm((F, 8, 4, 8, 128), f32),
            vm((F, 8, 4, 8, 128), f32),
            vm((F, 8, 4, 8, 128), f32),
            vm((F, 4, 4, 8, 128), f32),
            vm((F, 4, 8, 128), f32),
            vm((F, 4, 8, 128), f32),
            vm((REC + 1, F, CZ), f32),
            vm((NX * NZ, F, CZ), f32),
            vm((NX * NZ + 1, F, CZ), f32),
            vm((F * REC, CZ), f32),
            vm((1, 128), f32),
            vm((NX, 1, 128), f32),
            vm((1, 128), f32),
            vm((NZ, 1, 128), f32),
            vm((1, 128), i32),
            vm((REC, 128), i32),
            vm((F, REC, CZ), f32),
            vm((F, REC, CZ), f32),
            sm((1, 1, REC), i32),
            sm((1, 1, REC), i32),
            sm((1, 128), i32),
            sm((REC, 128), i32),
            dma((11,)),
            dma((2,)),
            dma((2,)),
            dma,
            dma,
            dma,
            dma,
            dma,
            dma,
            pltpu.SemaphoreType.REGULAR((3,)),
        ],
        compiler_params=pltpu.CompilerParams(collective_id=0, has_side_effects=True),
    )(
        fine_state,
        patch_ghosts,
        coarse_state[0, 0].transpose(1, 0, 2),
        coarse_face_term[0, 0].transpose(1, 0, 2),
        dest_grp,
        dest_column,
    )
    fine_new, coarse_new = pl.pallas_call(
        store_kernel,
        out_shape=(
            jax.ShapeDtypeStruct(fine_state.shape, f32),
            jax.ShapeDtypeStruct((F, REC, CZ), f32),
        ),
        in_specs=[vmem_spec] * 2,
        out_specs=(any_spec, any_spec),
        scratch_shapes=[dma((3,))],
    )(
        pltpu.with_memory_space_constraint(fine_new, vm),
        pltpu.with_memory_space_constraint(coarse_new, vm),
    )
    return fine_new, coarse_new.transpose(1, 0, 2)[None, None]


def solution(mesh):
    in_specs = (
        P("grp", None, "box", None, None),
        P("grp", None, None, None, None, None),
        P("grp", "box", None, None, None),
        P("grp", "box", None, None, None),
        P("grp", "box", None),
        P("grp", "box", None),
    )
    out_specs = (P("grp", None, "box", None, None), P("grp", "box", None, None, None))
    return jax.shard_map(
        on_device, mesh=mesh, in_specs=in_specs, out_specs=out_specs, check_vma=False
    )
```

time: 32.4 us -> 31.1 us (0.960)
  Pallas kernels: 31.7 us -> 30.3 us
    pallas_call x1, Pallas kernels: 30.9 us -> 29.5 us  [on_device(): pl.pallas_call(kernel, out_shape=(vm((F, 4, 2, 16, 128), f32), vm((F, REC...]
where the time goes in v3:
time: 31.1 us; the launch traced here: 30.9 us
  Pallas kernels  30.3 us (97%)
  between operations  0.64 us (2%)
    pallas_call x1, Pallas kernels, on_device(): pl.pallas_call(kernel, out_shape=(vm((F, 4, 2, 16, 128), f32), vm((F, REC...  29.5 us
    pallas_call x1, Pallas kernels, on_device(): pl.pallas_call(store_kernel, out_shape=(jax.ShapeDtypeStruct(fine_state.s...  0.77 us

profile of v3, /device:TPU:8, one launch (start us, length us, event | category | flops | bytes accessed | tf_op | source)
XLA Modules:
  0.0 30.9 jit_solution(6769436566691207750)
XLA Ops:
  0.6 29.5 %shard_map.77 = (f32[5,4,2,16,128]{4,3,2,1,0:T(8,128)S(1)}, f32[5,24,128]{2,1,0:T(8,128)S(1)}) custom-call(f32[1,5,4,16,256]{4,3,2,1,0:T(8,128)} %fine.1, f32[1,2,2,5,16,256]{5,4,3,2,1,0:T(8,128)} %ghosts.1, f32[5,24,128]{2,1,0:T(8,128)} %bitcast.9, f32[5,24,128]{2,1,0:T(8,128)} %bitcast.10, s32[1,1,24]{2,1,0:T(1,128)} %dgrp.1, s32[1,1,24]{2,1,0:T(1,128)} %dcol.1), custom_call_target="tpu_custom_call" | custom-call | tf_op jit(solution)/shard_map/pallas_call | solution.py:468
  30.2 0.8 %shard_map.78 = (f32[1,5,4,16,256]{4,3,2,1,0:T(8,128)}, f32[5,24,128]{2,1,0:T(8,128)}) custom-call(f32[5,4,2,16,128]{4,3,2,1,0:T(8,128)S(1)} %get-tuple-element.6.fine_v, f32[5,24,128]{2,1,0:T(8,128)S(1)} %get-tuple-element.7.coarse_v), custom_call_target="tpu_custom_call" | custom-call | tf_op jit(solution)/shard_map/pallas_call | solution.py:520

commit v4 on v3

--- a/solution.py
+++ b/solution.py
@@ -195,11 +195,18 @@
             device_id={"box": box + 1}, device_id_type=MESH,
         )
 
+    odd = lax.rem(box, 2) == 1
+    even = jnp.logical_not(odd)
+
+    @pl.when(even)
+    def _():
+        halo_up().start()
+
     @pl.when(jnp.logical_not(at_low))
     def _():
         halo_down().start()
 
-    @pl.when(jnp.logical_not(at_high))
+    @pl.when(odd & jnp.logical_not(at_high))
     def _():
         halo_up().start()
 
@@ -312,9 +319,6 @@
         def _():
             ghost_planes(1, 6, 7)
 
-    odd = lax.rem(box, 2) == 1
-    even = jnp.logical_not(odd)
-
     @pl.when(odd)
     def _():
         wait_low()
@@ -360,8 +364,6 @@
     for dx in range(1, NX):
         signal(hello.at[2], grp=peer(dx, 0))
     steps = [8, 7, 9, 6, 10, 5, 11, 4, 12, 3, 13, 2, 14, 1, 15]
-    for dz in steps:
-        send(bundle, code_z.at[mz], cz_s, cz_r, peer(0, dz)).start()
 
     second((jnp.where(odd, 5, 1), 2), (jnp.where(odd, 4, 1), 2), jnp.where(odd, 4, 2))
 
@@ -388,6 +390,9 @@
 
     pl.semaphore_wait(hello.at[2], NX - 1)
     for dz in steps + [0]:
+        if dz == 6:
+            for to_z in steps:
+                send(bundle, code_z.at[mz], cz_s, cz_r, peer(0, to_z)).start()
         for dx in (2, 1, 3, 0):
             if (dx, dz) != (0, 0):
                 to = peer(dx, dz)

time: 31.1 us -> 32.4 us (1.042)
  Pallas kernels: 30.3 us -> 31.7 us
    pallas_call x1, Pallas kernels: 29.5 us -> 30.9 us  [on_device(): pl.pallas_call(kernel, out_shape=(vm((F, 4, 2, 16, 128), f32), vm((F, REC...]
where the time goes in v4:
time: 32.4 us; the launch traced here: 32.3 us
  Pallas kernels  31.7 us (98%)
  between operations  0.64 us (2%)
    pallas_call x1, Pallas kernels, on_device(): pl.pallas_call(kernel, out_shape=(vm((F, 4, 2, 16, 128), f32), vm((F, REC...  30.9 us
    pallas_call x1, Pallas kernels, on_device(): pl.pallas_call(store_kernel, out_shape=(jax.ShapeDtypeStruct(fine_state.s...  0.77 us

profile of v4, /device:TPU:8, one launch (start us, length us, event | category | flops | bytes accessed | tf_op | source)
XLA Modules:
  0.0 32.3 jit_solution(15140265029142982007)
XLA Ops:
  0.6 30.9 %shard_map.77 = (f32[5,4,2,16,128]{4,3,2,1,0:T(8,128)S(1)}, f32[5,24,128]{2,1,0:T(8,128)S(1)}) custom-call(f32[1,5,4,16,256]{4,3,2,1,0:T(8,128)} %fine.1, f32[1,2,2,5,16,256]{5,4,3,2,1,0:T(8,128)} %ghosts.1, f32[5,24,128]{2,1,0:T(8,128)} %bitcast.9, f32[5,24,128]{2,1,0:T(8,128)} %bitcast.10, s32[1,1,24]{2,1,0:T(1,128)} %dgrp.1, s32[1,1,24]{2,1,0:T(1,128)} %dcol.1), custom_call_target="tpu_custom_call" | custom-call | tf_op jit(solution)/shard_map/pallas_call | solution.py:473
  31.5 0.8 %shard_map.78 = (f32[1,5,4,16,256]{4,3,2,1,0:T(8,128)}, f32[5,24,128]{2,1,0:T(8,128)}) custom-call(f32[5,4,2,16,128]{4,3,2,1,0:T(8,128)S(1)} %get-tuple-element.6.fine_v, f32[5,24,128]{2,1,0:T(8,128)S(1)} %get-tuple-element.7.coarse_v), custom_call_target="tpu_custom_call" | custom-call | tf_op jit(solution)/shard_map/pallas_call | solution.py:525

commit v5 on v4

--- a/solution.py
+++ b/solution.py
@@ -364,6 +364,8 @@
     for dx in range(1, NX):
         signal(hello.at[2], grp=peer(dx, 0))
     steps = [8, 7, 9, 6, 10, 5, 11, 4, 12, 3, 13, 2, 14, 1, 15]
+    for dz in steps:
+        send(bundle, code_z.at[mz], cz_s, cz_r, peer(0, dz)).start()
 
     second((jnp.where(odd, 5, 1), 2), (jnp.where(odd, 4, 1), 2), jnp.where(odd, 4, 2))
 
@@ -390,9 +392,6 @@
 
     pl.semaphore_wait(hello.at[2], NX - 1)
     for dz in steps + [0]:
-        if dz == 6:
-            for to_z in steps:
-                send(bundle, code_z.at[mz], cz_s, cz_r, peer(0, to_z)).start()
         for dx in (2, 1, 3, 0):
             if (dx, dz) != (0, 0):
                 to = peer(dx, dz)

time: 32.4 us -> 31.1 us (0.960)
  Pallas kernels: 31.7 us -> 30.3 us
    pallas_call x1, Pallas kernels: 30.9 us -> 29.5 us  [on_device(): pl.pallas_call(kernel, out_shape=(vm((F, 4, 2, 16, 128), f32), vm((F, REC...]
where the time goes in v5:
time: 31.1 us; the launch traced here: 30.9 us
  Pallas kernels  30.3 us (97%)
  between operations  0.64 us (2%)
    pallas_call x1, Pallas kernels, on_device(): pl.pallas_call(kernel, out_shape=(vm((F, 4, 2, 16, 128), f32), vm((F, REC...  29.5 us
    pallas_call x1, Pallas kernels, on_device(): pl.pallas_call(store_kernel, out_shape=(jax.ShapeDtypeStruct(fine_state.s...  0.77 us

profile of v5, /device:TPU:8, one launch (start us, length us, event | category | flops | bytes accessed | tf_op | source)
XLA Modules:
  0.0 30.9 jit_solution(3389456402940012464)
XLA Ops:
  0.6 29.5 %shard_map.77 = (f32[5,4,2,16,128]{4,3,2,1,0:T(8,128)S(1)}, f32[5,24,128]{2,1,0:T(8,128)S(1)}) custom-call(f32[1,5,4,16,256]{4,3,2,1,0:T(8,128)} %fine.1, f32[1,2,2,5,16,256]{5,4,3,2,1,0:T(8,128)} %ghosts.1, f32[5,24,128]{2,1,0:T(8,128)} %bitcast.9, f32[5,24,128]{2,1,0:T(8,128)} %bitcast.10, s32[1,1,24]{2,1,0:T(1,128)} %dgrp.1, s32[1,1,24]{2,1,0:T(1,128)} %dcol.1), custom_call_target="tpu_custom_call" | custom-call | tf_op jit(solution)/shard_map/pallas_call | solution.py:472
  30.2 0.8 %shard_map.78 = (f32[1,5,4,16,256]{4,3,2,1,0:T(8,128)}, f32[5,24,128]{2,1,0:T(8,128)}) custom-call(f32[5,4,2,16,128]{4,3,2,1,0:T(8,128)S(1)} %get-tuple-element.6.fine_v, f32[5,24,128]{2,1,0:T(8,128)S(1)} %get-tuple-element.7.coarse_v), custom_call_target="tpu_custom_call" | custom-call | tf_op jit(solution)/shard_map/pallas_call | solution.py:524
